TPU v7x, 32 devices: a whole 2x2x4 slice. The times are simulated.
32 devices in a mesh: grp: 2 (over x), filt: 8 (over z, y), sky: 2 (over core).
Axes of the slice: x: 2, y: 2, z: 4, core: 2. Of those that a mesh axis runs over, the one named last changes fastest.
Arguments:
- strain: bfloat16 [2, 6, 524288], P(None, 'grp', 'filt'), parts along dimension 1, may hold values from -4 to 4
- templates: bfloat16 [2, 4, 524288], P(None, 'sky', 'filt'), may hold values from -6 to 6
- lengths: int32 [4], P('sky'), may hold values from 131072 to 524288
- antenna: bfloat16 [2, 3, 3072], P(None, None, 'sky'), may hold values from -1 to 1
- delays: int32 [3, 3072], P(None, 'sky'), may hold values from -48 to 48
Outputs:
- peak: float32 [2, 2048, 3072], P('grp', 'filt', 'sky'), parts along dimension 0
There are 2 independent parts, one for each index of `grp`. A program takes and returns all parts, laid end to end along the dimension named above; an argument that names none is the same for every part. Nothing has to cross between parts.
All inputs are finite; a program needn't handle non-finite values.
Results may differ from a plain program's by a relative error of at most 0.018.
Values may be sent and summed in bfloat16 or wider, within the bound.
No kernel may reach another device: no remote copies, remote signals or barrier semaphores. Data moves between devices by JAX's collectives and lax.ppermute only.
A program may use at most 64 MiB of HBM per device.

v0:
```python
import functools

import jax
import jax.numpy as jnp
import numpy as np
from jax import lax
from jax.experimental import pallas as pl
from jax.experimental.pallas import tpu as pltpu
from jax.sharding import PartitionSpec as P

N1 = 2048
N2 = 512
DM = 48
K2 = 3
LANES = 128
ROWS = 16


def turn(phase):
    angle = 2.0 * np.pi * (phase - np.floor(phase))
    return np.stack([np.cos(angle), np.sin(angle)]).astype(np.float32)


def tables(depth, rows, whole_length, half_tiles, devices):
    centre2 = 2 * (2 * N1 + DM) - 2 * half_tiles * LANES - 1
    row = np.arange(rows, dtype=np.int64)[:, None]
    col = np.arange(depth, dtype=np.int64)[None, :]
    odd = 2 * np.arange(LANES, dtype=np.int64)[None, :] + 1
    turns = 2 * whole_length
    start = turn(((row * depth + col) * centre2 % turns) / turns)
    col_first = turn((col.T * odd % turns) / turns)
    col_step = turn((col.T * (2 * LANES) % turns) / turns * np.ones((1, LANES)))
    row_first = turn((row * depth * odd % turns) / turns)
    row_step = turn((row * depth * (2 * LANES) % turns) / turns * np.ones((1, LANES)))
    pos = np.arange(devices, dtype=np.int64)[:, None]
    t_up = (centre2 + odd) // 2
    t_down = (centre2 - odd) // 2
    base = rows * depth
    up = turn((pos * base * t_up % whole_length) / whole_length)
    down = turn((pos * base * t_down % whole_length) / whole_length)
    offset = np.concatenate([up, down]).transpose(1, 0, 2)
    flip = np.eye(LANES, dtype=np.float32)[::-1]
    return start, col_first, col_step, row_first, row_step, offset, flip


def series_kernel(
    temps, dets, own, devices, copies, half_tiles,
    lengths, strain, templates, start, col_first, col_step, row_first, row_step, offset, flip,
    out, spectra, sums_a, sums_b, col_now, row_now, series,
):
    rows, depth = strain.shape[2], strain.shape[3]
    count = temps * dets
    pos = lax.axis_index("filt")
    chunk = 16
    norms = [jnp.zeros((chunk, depth), jnp.float32) for _ in range(temps)]

    def filter_chunk(step, norms):
        first = pl.multiple_of(step * chunk, chunk)
        here = pl.ds(first, chunk)
        bins = (
            (pos * rows + first) * depth
            + lax.broadcasted_iota(jnp.int32, (chunk, depth), 0) * depth
            + lax.broadcasted_iota(jnp.int32, (chunk, depth), 1)
        )
        s_re = [strain[0, d, here, :].astype(jnp.float32) for d in range(dets)]
        s_im = [strain[1, d, here, :].astype(jnp.float32) for d in range(dets)]
        p_re, p_im = start[0, here, :], start[1, here, :]
        added = []
        for k in range(temps):
            inside = bins < lengths[k]
            h_re = jnp.where(inside, templates[0, k, here, :].astype(jnp.float32), 0.0)
            h_im = jnp.where(inside, templates[1, k, here, :].astype(jnp.float32), 0.0)
            added.append(norms[k] + (h_re * h_re + h_im * h_im))
            g_re = h_re * p_re + h_im * p_im
            g_im = h_re * p_im - h_im * p_re
            for d in range(dets):
                q = k * dets + d
                x_re = g_re * s_re[d] - g_im * s_im[d]
                x_im = g_re * s_im[d] + g_im * s_re[d]
                spectra[pl.ds(pl.multiple_of(q * rows + first, chunk), chunk), :] = x_re.astype(jnp.bfloat16)
                spectra[pl.ds(pl.multiple_of((count + q) * rows + first, chunk), chunk), :] = x_im.astype(
                    jnp.bfloat16
                )
        return added

    norms = lax.fori_loop(0, rows // chunk, filter_chunk, norms)
    high, low = [], []
    for k in range(temps):
        total = jnp.sum(jnp.sum(norms[k], axis=0, keepdims=True), axis=1, keepdims=True)
        total = jnp.broadcast_to(total, (1, LANES))
        first = total.astype(jnp.bfloat16).astype(jnp.float32)
        high.append(first)
        low.append(total - first)
    f_ur, f_ui, f_dr, f_di = (offset[pos, i : i + 1, :] for i in range(4))

    col_now[...] = col_first[...]
    row_now[...] = row_first[...]

    def section(sums):
        c_re, c_im = col_now[0], col_now[1]
        table = jnp.concatenate([c_re, c_im], axis=1).astype(jnp.bfloat16)
        sums[...] = jnp.dot(spectra[...], table, preferred_element_type=jnp.float32)
        d_re, d_im = col_step[0], col_step[1]
        col_now[0] = c_re * d_re - c_im * d_im
        col_now[1] = c_re * d_im + c_im * d_re

    def collect(sums, tile):
        w_re, w_im = row_now[0], row_now[1]
        up_re, up_im, down_re, down_im = [], [], [], []
        for q in range(count):
            top, low_rows = pl.ds(q * rows, rows), pl.ds((count + q) * rows, rows)
            a, d = sums[top, :LANES], sums[top, LANES:]
            e, b = sums[low_rows, :LANES], sums[low_rows, LANES:]
            s1 = jnp.sum(a * w_re - d * w_im, axis=0, keepdims=True)
            s2 = jnp.sum(b * w_re + e * w_im, axis=0, keepdims=True)
            s3 = jnp.sum(e * w_re - b * w_im, axis=0, keepdims=True)
            s4 = jnp.sum(d * w_re + a * w_im, axis=0, keepdims=True)
            r, i = s1 - s2, s3 + s4
            up_re.append(r * f_ur - i * f_ui)
            up_im.append(r * f_ui + i * f_ur)
            r, i = s1 + s2, s3 - s4
            down_re.append(r * f_dr - i * f_di)
            down_im.append(r * f_di + i * f_dr)
        upper = jnp.concatenate(up_re + high + up_im + low, axis=0).astype(jnp.bfloat16)
        lower = jnp.concatenate(down_re + high + down_im + low, axis=0).astype(jnp.bfloat16)
        upper = jnp.dot(upper, flip[...], preferred_element_type=jnp.float32).astype(jnp.bfloat16)
        series[:, pl.ds(pl.multiple_of((half_tiles - 1 - tile) * LANES, LANES), LANES)] = upper
        series[:, pl.ds(pl.multiple_of((half_tiles + tile) * LANES, LANES), LANES)] = lower
        d_re, d_im = row_step[0], row_step[1]
        row_now[0] = w_re * d_re - w_im * d_im
        row_now[1] = w_re * d_im + w_im * d_re

    section(sums_a)

    def pair(step, carry):
        section(sums_b)
        collect(sums_a, 2 * step)
        section(sums_a)
        collect(sums_b, 2 * step + 1)
        return carry

    pairs = (half_tiles - 1) // 2
    lax.fori_loop(0, pairs, pair, 0)
    if half_tiles % 2:
        collect(sums_a, half_tiles - 1)
    else:
        section(sums_b)
        collect(sums_a, half_tiles - 2)
        collect(sums_b, half_tiles - 1)

    width = out.shape[2]
    for target in range(devices):
        first = own * (devices - 1 - target)
        window = series[:, first : first + width]
        for copy in range(copies):
            out[target * copies + copy] = window


def sky_kernel(temps, dets, own, sources, copies, received, delays, antenna, out, hankel, weights):
    width = received.shape[2]
    sky = delays.shape[1]
    tile = 2 * LANES
    lag = DM - lax.broadcasted_iota(jnp.int32, (LANES, sky), 0)
    for d in range(dets):
        hit = lag == delays[d : d + 1, :]
        for p in range(2):
            value = jnp.where(hit, antenna[p, d : d + 1, :].astype(jnp.float32), 0.0).astype(jnp.bfloat16)
            for i in range(sky // tile):
                weights[i, d * LANES : (d + 1) * LANES, p * tile : (p + 1) * tile] = value[:, i * tile : (i + 1) * tile]
    count = temps * dets
    block = min(own, LANES)
    for c in range(copies):
        total = received[c].astype(jnp.float32)
        for source in range(1, sources):
            total = total + received[source * copies + c].astype(jnp.float32)
        scales = []
        for k in range(temps):
            norm = total[count + k : count + k + 1] + total[ROWS // 2 + count + k : ROWS // 2 + count + k + 1]
            scales.append(lax.rsqrt(norm + 1e-06))
        for k in range(temps):
            for part in range(2):
                for d in range(dets):
                    row = part * (ROWS // 2) + k * dets + d
                    line = (total[row : row + 1] * scales[k]).astype(jnp.bfloat16).astype(jnp.float32)
                    for first in range(0, own, block):
                        start = own - block - first
                        piece = jnp.broadcast_to(line[:, start : start + 2 * LANES], (block, 2 * LANES))
                        moved = pltpu.roll(piece, 2 * LANES + 1 - block, 1, stride=1, stride_axis=0)
                        hankel[
                            c * temps + k, part * own + first : part * own + first + block, d * LANES : (d + 1) * LANES
                        ] = moved[:, :LANES].astype(jnp.bfloat16)

    def sky_tile(i, carry):
        best = None
        for k in range(copies * temps):
            mixed = jnp.dot(hankel[k], weights[i], preferred_element_type=jnp.float32)
            power = mixed * mixed
            power = power[:own] + power[own:]
            power = power[:, :tile] + power[:, tile:]
            best = power if best is None else jnp.maximum(best, power)
        out[:, pl.ds(pl.multiple_of(i * tile, tile), tile)] = best
        return carry

    lax.fori_loop(0, sky // tile, sky_tile, 0)


def body(strain, templates, lengths, antenna, delays):
    devices = lax.axis_size("filt")
    copies = lax.axis_size("sky")
    temps, dets, bins = templates.shape[1], strain.shape[1], strain.shape[2]
    sky = delays.shape[1]
    depth = N2
    rows = bins // depth
    whole_length = 2 * bins * devices
    own = N1 // devices
    span = N1 + 2 * DM
    half_tiles = -(-span // (2 * LANES))
    width = -(-own // LANES) * LANES + LANES
    tabs = tables(depth, rows, whole_length, half_tiles, devices)
    start, col_first, col_step, row_first, row_step, offset = (jnp.asarray(t) for t in tabs[:6])
    flip = jnp.asarray(tabs[6], jnp.bfloat16)
    count = temps * dets
    vmem = pl.BlockSpec(memory_space=pltpu.VMEM)
    smem = pl.BlockSpec(memory_space=pltpu.SMEM)
    shaped_s = strain.reshape(2, dets, rows, depth)
    shaped_h = templates.reshape(2, temps, rows, depth)
    parts = pl.pallas_call(
        functools.partial(series_kernel, temps, dets, own, devices, copies, half_tiles),
        out_shape=jax.ShapeDtypeStruct((devices * copies, ROWS, width), jnp.bfloat16),
        in_specs=[smem] + [vmem] * 9,
        out_specs=vmem,
        scratch_shapes=[
            pltpu.VMEM((2 * count * rows, depth), jnp.bfloat16),
            pltpu.VMEM((2 * count * rows, 2 * LANES), jnp.float32),
            pltpu.VMEM((2 * count * rows, 2 * LANES), jnp.float32),
            pltpu.VMEM((2, depth, LANES), jnp.float32),
            pltpu.VMEM((2, rows, LANES), jnp.float32),
            pltpu.VMEM((ROWS, 2 * half_tiles * LANES), jnp.bfloat16),
        ],
        compiler_params=pltpu.CompilerParams(vmem_limit_bytes=48 << 20),
        name="series",
    )(lengths, shaped_s, shaped_h, start, col_first, col_step, row_first, row_step, offset, flip)
    received = lax.all_to_all(parts, ("filt", "sky"), split_axis=0, concat_axis=0, tiled=True)
    best = pl.pallas_call(
        functools.partial(sky_kernel, temps, dets, own, devices, copies),
        out_shape=jax.ShapeDtypeStruct((own, sky), jnp.float32),
        in_specs=[vmem] * 3,
        out_specs=vmem,
        scratch_shapes=[
            pltpu.VMEM((copies * temps, 2 * own, dets * LANES), jnp.bfloat16),
            pltpu.VMEM((sky // (2 * LANES), dets * LANES, 4 * LANES), jnp.bfloat16),
        ],
        compiler_params=pltpu.CompilerParams(vmem_limit_bytes=48 << 20),
        name="sky",
    )(received, delays, antenna)
    return best[None]


def solution(mesh):
    in_specs = (
        P(None, "grp", "filt"),
        P(None, "sky", "filt"),
        P("sky"),
        P(None, None, "sky"),
        P(None, "sky"),
    )
    out_specs = P("grp", "filt", "sky")
    return jax.shard_map(body, mesh=mesh, in_specs=in_specs, out_specs=out_specs, check_vma=False)
```

profile of v0, /device:TPU:0, one launch (start us, length us, event | category | flops | bytes accessed | tf_op | source)
XLA Modules:
  0.0 38.9 jit_solution(2211935309046410645)
XLA Ops:
  0.0 2.3 %reshape.6 = bf16[2,3,128,512]{3,2,0,1:T(8,128)(2,1)S(1)} reshape(bf16[2,3,65536]{2,0,1:T(2,128)(2,1)} %param.12) | data formatting | bytes 1572864 | tf_op jit(solution)/shard_map/reshape | solution.py:225
  2.3 0.0 copy-start
  2.3 0.0 copy-start.1
  2.3 0.0 copy-start.2
  2.4 0.0 copy-start.3
  2.4 0.0 copy-start.4
  2.4 0.0 copy-start.5
  2.4 0.0 copy-start.7
  2.4 0.0 copy-start.8
  2.4 0.1 copy.15.strain
  2.5 1.5 %reshape.7.templates = bf16[2,2,128,512]{3,2,1,0:T(8,128)(2,1)S(1)} reshape(bf16[2,2,65536]{2,1,0:T(2,128)(2,1)} %param.13) | data formatting | bytes 1048576 | tf_op jit(solution)/shard_map/reshape | solution.py:226
  4.0 0.0 copy-done
  4.0 0.0 copy-done.1
  4.0 0.0 copy-done.2
  4.0 0.0 copy-done.3
  4.0 0.0 copy-done.4
  4.0 0.0 copy-done.5
  4.0 0.0 copy-done.7
  4.0 0.0 copy-start.9
  4.1 0.0 copy-start.6
  4.1 8.5 %series.1 = bf16[16,16,384]{2,1,0:T(8,128)(2,1)} custom-call(s32[2]{0:T(128)S(1)} %copy-done.8, bf16[2,3,128,512]{3,2,1,0:T(8,128)(2,1)S(1)} %copy.15.strain, bf16[2,2,128,512]{3,2,1,0:T(8,128)(2,1)S(1)} %reshape.7.templates, f32[2,128,512]{2,1,0:T(8,128)S(1)} %copy-done, f32[2,512,128]{2,1,0:T(8,128)S(1)} %copy-done.1, f32[2,512,128]{2,1,0:T(8,128)S(1)} %copy-done.2, ...), custom_call_target="tpu_custom_call" | custom-call | tf_op jit(solution)/shard_map/series/pallas_call | solution.py:227
  12.6 7.4 %all-to-all-start = ((bf16[16,16,384]{2,1,0:T(8,128)(2,1)}), bf16[16,16,384]{2,1,0:T(8,128)(2,1)S(1)}, u32[]{:S(2)}, u32[]{:S(2)}) async-start(bf16[16,16,384]{2,1,0:T(8,128)(2,1)} %series.1), calls=%async_computation | async-start | bytes 393216 | tf_op jit(solution)/shard_map/all_to_all | solution.py:243
  20.0 8.9 %all-to-all-done.received = bf16[16,16,384]{2,1,0:T(8,128)(2,1)S(1)} async-done(((bf16[16,16,384]{2,1,0:T(8,128)(2,1)}), bf16[16,16,384]{2,1,0:T(8,128)(2,1)S(1)}, u32[]{:S(2)}, u32[]{:S(2)}) %all-to-all-start) | async-done | bytes 196640 | tf_op jit(solution)/shard_map/all_to_all | solution.py:243
  28.9 10.0 %sky.1 = f32[256,1536]{1,0:T(8,128)} custom-call(bf16[16,16,384]{2,1,0:T(8,128)(2,1)S(1)} %all-to-all-done.received, s32[3,1536]{1,0:T(4,128)S(1)} %copy-done.6, bf16[2,3,1536]{2,1,0:T(4,128)(2,1)S(1)} %copy.16.antenna), custom_call_target="tpu_custom_call" | custom-call | tf_op jit(solution)/shard_map/sky/pallas_call | solution.py:244
  (4 shorter events, 0.0 us)
Async XLA Ops:
  2.3 1.6 %copy-start = (f32[2,128,512]{2,1,0:T(8,128)S(1)}, f32[2,128,512]{2,1,0:T(8,128)}, u32[]{:S(2)}) copy-start(f32[2,128,512]{2,1,0:T(8,128)} %constant.14.clone.start) | copy-start | bytes 1572868
  2.3 1.6 %copy-start.1 = (f32[2,512,128]{2,1,0:T(8,128)S(1)}, f32[2,512,128]{2,1,0:T(8,128)}, u32[]{:S(2)}) copy-start(f32[2,512,128]{2,1,0:T(8,128)} %constant.15.clone.col_first) | copy-start | bytes 1572868
  2.3 1.6 %copy-start.2 = (f32[2,512,128]{2,1,0:T(8,128)S(1)}, f32[2,512,128]{2,1,0:T(8,128)}, u32[]{:S(2)}) copy-start(f32[2,512,128]{2,1,0:T(8,128)} %constant.16.clone.col_step) | copy-start | bytes 1572868
  2.4 1.6 %copy-start.3 = (f32[2,128,128]{2,1,0:T(8,128)S(1)}, f32[2,128,128]{2,1,0:T(8,128)}, u32[]{:S(2)}) copy-start(f32[2,128,128]{2,1,0:T(8,128)} %constant.17.clone.row_first) | copy-start | bytes 393220
  2.4 1.6 %copy-start.4 = (f32[2,128,128]{2,1,0:T(8,128)S(1)}, f32[2,128,128]{2,1,0:T(8,128)}, u32[]{:S(2)}) copy-start(f32[2,128,128]{2,1,0:T(8,128)} %constant.18.clone.row_step) | copy-start | bytes 393220
  2.4 1.6 %copy-start.5 = (bf16[128,128]{1,0:T(8,128)(2,1)S(1)}, bf16[128,128]{1,0:T(8,128)(2,1)}, u32[]{:S(2)}) copy-start(bf16[128,128]{1,0:T(8,128)(2,1)} %constant.20.clone.flip) | copy-start | bytes 98308
  2.4 1.6 %copy-start.7 = (f32[8,4,128]{2,1,0:T(4,128)S(1)}, f32[8,4,128]{2,1,0:T(4,128)}, u32[]{:S(2)}) copy-start(f32[8,4,128]{2,1,0:T(4,128)} %constant.19.clone.offset) | copy-start | bytes 49156
  2.4 1.6 %copy-start.8 = (s32[2]{0:T(128)S(1)}, s32[2]{0:T(128)}, u32[]{:S(2)}) copy-start(s32[2]{0:T(128)} %lengths.1) | copy-start | bytes 28
  4.0 15.9 %copy-start.9 = (bf16[2,3,1536]{2,0,1:T(2,128)(2,1)S(1)}, bf16[2,3,1536]{2,0,1:T(2,128)(2,1)}, u32[]{:S(2)}) copy-start(bf16[2,3,1536]{2,0,1:T(2,128)(2,1)} %param.15) | copy-start | bytes 55300
  4.1 24.9 %copy-start.6 = (s32[3,1536]{1,0:T(4,128)S(1)}, s32[3,1536]{1,0:T(4,128)}, u32[]{:S(2)}) copy-start(s32[3,1536]{1,0:T(4,128)} %delays.1) | copy-start | bytes 55300
  12.6 16.4 %all-to-all-start = ((bf16[16,16,384]{2,1,0:T(8,128)(2,1)}), bf16[16,16,384]{2,1,0:T(8,128)(2,1)S(1)}, u32[]{:S(2)}, u32[]{:S(2)}) async-start(bf16[16,16,384]{2,1,0:T(8,128)(2,1)} %series.1), calls=%async_computation | async-start | bytes 393216 | tf_op jit(solution)/shard_map/all_to_all | solution.py:243
where the time goes:
time: 39.2 us; the launch traced here: 38.9 us
  Pallas kernels  18.4 us (47%)
  waiting for transfers between devices  8.93 us (23%)
  starting transfers between devices  7.41 us (19%)
  local copies, waits for them, and re-layouts  3.92 us (10%)
    pallas_call x1, Pallas kernels, body(): pl.pallas_call(functools.partial(sky_kernel, temps, dets, own, devices, c...  9.96 us
    all_to_all x1, waiting for transfers between devices, body(): lax.all_to_all(parts, ('filt', 'sky'), split_axis=0, concat_axis=0, tiled...  8.93 us
    pallas_call x1, Pallas kernels, body(): pl.pallas_call(functools.partial(series_kernel, temps, dets, own, devices...  8.48 us
    all_to_all x1, starting transfers between devices, body(): lax.all_to_all(parts, ('filt', 'sky'), split_axis=0, concat_axis=0, tiled...  7.41 us
    reshape x2, local copies, waits for them, and re-layouts, body(): shaped_s = strain.reshape(2, dets, rows, depth)  2.36 us
    reshape x1, local copies, waits for them, and re-layouts, body(): shaped_h = templates.reshape(2, temps, rows, depth)  1.48 us
  transfers between devices with their start and end apart: 1, of which 1 were waited for; matrix products, arithmetic and copies ran while one was open for 0% of the time, Pallas kernels for 0%

commit v1 on v0

v1 whole, which is shorter than its diff:
```python
import functools

import jax
import jax.numpy as jnp
import numpy as np
from jax import lax
from jax.experimental import pallas as pl
from jax.experimental.pallas import tpu as pltpu
from jax.sharding import PartitionSpec as P

N1 = 2048
N2 = 512
DM = 48
K2 = 3
LANES = 128
ROWS = 16


def turn(phase):
    angle = 2.0 * np.pi * (phase - np.floor(phase))
    return np.stack([np.cos(angle), np.sin(angle)]).astype(np.float32)


def tables(depth, rows, whole_length, half_tiles, devices):
    centre2 = 2 * (2 * N1 + DM) - 2 * half_tiles * LANES - 1
    row = np.arange(rows, dtype=np.int64)[:, None]
    col = np.arange(depth, dtype=np.int64)[None, :]
    odd = 2 * np.arange(LANES, dtype=np.int64)[None, :] + 1
    turns = 2 * whole_length
    start = turn(((row * depth + col) * centre2 % turns) / turns)
    col_first = turn((col.T * odd % turns) / turns)
    col_step = turn((col.T * (2 * LANES) % turns) / turns * np.ones((1, LANES)))
    row_first = turn((row * depth * odd % turns) / turns)
    row_step = turn((row * depth * (2 * LANES) % turns) / turns * np.ones((1, LANES)))
    pos = np.arange(devices, dtype=np.int64)[:, None]
    t_up = (centre2 + odd) // 2
    t_down = (centre2 - odd) // 2
    base = rows * depth
    up = turn((pos * base * t_up % whole_length) / whole_length)
    down = turn((pos * base * t_down % whole_length) / whole_length)
    offset = np.concatenate([up, down]).transpose(1, 0, 2)
    flip = np.eye(LANES, dtype=np.float32)[::-1]
    return start, col_first, col_step, row_first, row_step, offset, flip


def series_kernel(
    temps, dets, own, devices, copies, half_tiles, together,
    lengths, strain, templates, start, col_first, col_step, row_first, row_step, offset, flip,
    out, spectra, col_now, row_now, series,
):
    rows, depth = strain.shape[2], strain.shape[3]
    count = temps * dets
    pos = lax.axis_index("filt")
    norms = [jnp.zeros((ROWS, depth), jnp.float32) for _ in range(temps)]

    def filter_chunk(step, norms):
        first = pl.multiple_of(step * ROWS, ROWS)
        here = pl.ds(first, ROWS)
        bins = (
            (pos * rows + first) * depth
            + lax.broadcasted_iota(jnp.int32, (ROWS, depth), 0) * depth
            + lax.broadcasted_iota(jnp.int32, (ROWS, depth), 1)
        )
        s_re = [strain[0, d, here, :].astype(jnp.float32) for d in range(dets)]
        s_im = [strain[1, d, here, :].astype(jnp.float32) for d in range(dets)]
        p_re, p_im = start[0, here, :], start[1, here, :]
        added = []
        for k in range(temps):
            inside = bins < lengths[k]
            h_re = jnp.where(inside, templates[0, k, here, :].astype(jnp.float32), 0.0)
            h_im = jnp.where(inside, templates[1, k, here, :].astype(jnp.float32), 0.0)
            added.append(norms[k] + (h_re * h_re + h_im * h_im))
            g_re = h_re * p_re + h_im * p_im
            g_im = h_re * p_im - h_im * p_re
            for d in range(dets):
                place = 2 * ((k * dets + d) * rows + first)
                x_re = g_re * s_re[d] - g_im * s_im[d]
                x_im = g_re * s_im[d] + g_im * s_re[d]
                spectra[pl.ds(pl.multiple_of(place, ROWS), ROWS), :] = x_re.astype(jnp.bfloat16)
                spectra[pl.ds(pl.multiple_of(place + ROWS, ROWS), ROWS), :] = x_im.astype(jnp.bfloat16)
        return added

    norms = lax.fori_loop(0, rows // ROWS, filter_chunk, norms)
    high, low = [], []
    for k in range(temps):
        total = jnp.sum(jnp.sum(norms[k], axis=0, keepdims=True), axis=1, keepdims=True)
        total = jnp.broadcast_to(total, (1, LANES))
        first = total.astype(jnp.bfloat16).astype(jnp.float32)
        high.append(first)
        low.append(total - first)
    f_ur, f_ui, f_dr, f_di = (offset[pos, i : i + 1, :] for i in range(4))

    col_now[...] = col_first[...]
    row_now[...] = row_first[...]

    def section(tile):
        c_re, c_im = col_now[0], col_now[1]
        table = jnp.concatenate([c_re, c_im], axis=1).astype(jnp.bfloat16)
        d_re, d_im = col_step[0], col_step[1]
        col_now[0] = c_re * d_re - c_im * d_im
        col_now[1] = c_re * d_im + c_im * d_re
        parts = 2
        height = spectra.shape[0] // parts
        pieces = [
            jnp.dot(spectra[i * height : (i + 1) * height, :], table, preferred_element_type=jnp.float32)
            for i in range(parts)
        ]
        up_re, up_im, down_re, down_im = [], [], [], []
        for q in range(count):
            s1 = s2 = s3 = s4 = None
            for block in range(0, rows, ROWS):
                place = 2 * (q * rows + block)
                for half in range(0, ROWS, 8):
                    w_re = row_now[0, block + half : block + half + 8, :]
                    w_im = row_now[1, block + half : block + half + 8, :]
                    sums = pieces[place // height]
                    top, end = place % height + half, place % height + ROWS + half
                    a, d = sums[top : top + 8, :LANES], sums[top : top + 8, LANES:]
                    e, b = sums[end : end + 8, :LANES], sums[end : end + 8, LANES:]
                    n1, n2 = a * w_re - d * w_im, b * w_re + e * w_im
                    n3, n4 = e * w_re - b * w_im, d * w_re + a * w_im
                    s1 = n1 if s1 is None else s1 + n1
                    s2 = n2 if s2 is None else s2 + n2
                    s3 = n3 if s3 is None else s3 + n3
                    s4 = n4 if s4 is None else s4 + n4
            r = jnp.sum(s1 - s2, axis=0, keepdims=True)
            i = jnp.sum(s3 + s4, axis=0, keepdims=True)
            up_re.append(r * f_ur - i * f_ui)
            up_im.append(r * f_ui + i * f_ur)
            r = jnp.sum(s1 + s2, axis=0, keepdims=True)
            i = jnp.sum(s3 - s4, axis=0, keepdims=True)
            down_re.append(r * f_dr - i * f_di)
            down_im.append(r * f_di + i * f_dr)
        upper = jnp.concatenate(up_re + high + up_im + low, axis=0).astype(jnp.bfloat16)
        lower = jnp.concatenate(down_re + high + down_im + low, axis=0).astype(jnp.bfloat16)
        upper = jnp.dot(upper, flip[...], preferred_element_type=jnp.float32).astype(jnp.bfloat16)
        series[:, pl.ds(pl.multiple_of((half_tiles - 1 - tile) * LANES, LANES), LANES)] = upper
        series[:, pl.ds(pl.multiple_of((half_tiles + tile) * LANES, LANES), LANES)] = lower
        w_re, w_im = row_now[0], row_now[1]
        d_re, d_im = row_step[0], row_step[1]
        row_now[0] = w_re * d_re - w_im * d_im
        row_now[1] = w_re * d_im + w_im * d_re

    def some(step, carry):
        for sub in range(together):
            section(step * together + sub)
        return carry

    lax.fori_loop(0, half_tiles // together, some, 0)

    width = out.shape[2]
    for target in range(devices):
        first = own * (devices - 1 - target)
        window = series[:, first : first + width]
        for copy in range(copies):
            out[target * copies + copy] = window


def weight_kernel(dets, delays, antenna, weights):
    tile = 2 * LANES
    sky = delays.shape[1]
    lag = DM - lax.broadcasted_iota(jnp.int32, (LANES, tile), 0)
    for i in range(sky // tile):
        part = slice(i * tile, (i + 1) * tile)
        for d in range(dets):
            hit = lag == delays[d : d + 1, part]
            for p in range(2):
                value = jnp.where(hit, antenna[p, d : d + 1, part].astype(jnp.float32), 0.0)
                weights[i, d * LANES : (d + 1) * LANES, p * tile : (p + 1) * tile] = value.astype(jnp.bfloat16)


def sky_kernel(temps, dets, own, sources, copies, received, weights, out, hankel):
    width = received.shape[2]
    tile = 2 * LANES
    count = temps * dets
    blocks = -(-own // LANES)
    groups = 2 * copies * temps

    @pl.when(pl.program_id(0) == 0)
    def _():
        for c in range(copies):
            total = received[c].astype(jnp.float32)
            for source in range(1, sources):
                total = total + received[source * copies + c].astype(jnp.float32)
            half = ROWS // 2
            for k in range(temps):
                norm = total[count + k : count + k + 1] + total[half + count + k : half + count + k + 1]
                scale = lax.rsqrt(norm + 1e-06)
                lines = []
                for part in range(2):
                    for d in range(dets):
                        row = part * half + k * dets + d
                        line = (total[row : row + 1] * scale).astype(jnp.bfloat16).astype(jnp.float32)
                        lines.append(
                            pltpu.roll(jnp.broadcast_to(line, (8, width)), 0, 1, stride=1, stride_axis=0)
                        )
                base = jnp.concatenate(lines, axis=0)
                for first in range(0, min(own, LANES), ROWS):
                    moved = [
                        pltpu.roll(base, (t + 1 - own + (blocks - 1) * LANES) % width, 1) for t in (first, first + 8)
                    ]
                    for part in range(2):
                        group = 2 * (c * temps + k) + part
                        for d in range(dets):
                            row = 8 * (part * dets + d)
                            for block in range(blocks):
                                lane = (blocks - 1 - block) * LANES
                                piece = jnp.concatenate([m[row : row + 8, lane : lane + LANES] for m in moved], axis=0)
                                place = ((block * LANES + first) // ROWS * groups + group) * ROWS
                                hankel[place : place + ROWS, d * LANES : (d + 1) * LANES] = piece.astype(jnp.bfloat16)

    span = min(128, own)
    for first in range(0, own, ROWS):
        if first % span == 0:
            mixed = jnp.dot(
                hankel[first * groups : (first + span) * groups, :], weights[0], preferred_element_type=jnp.float32
            )
        best = None
        for k in range(copies * temps):
            place = first % span * groups + 2 * k * ROWS
            re, im = mixed[place : place + ROWS], mixed[place + ROWS : place + 2 * ROWS]
            power = re * re + im * im
            power = power[:, :tile] + power[:, tile:]
            best = power if best is None else jnp.maximum(best, power)
        out[first : first + ROWS, :] = best


def body(strain, templates, lengths, antenna, delays):
    devices = lax.axis_size("filt")
    copies = lax.axis_size("sky")
    temps, dets, bins = templates.shape[1], strain.shape[1], strain.shape[2]
    sky = delays.shape[1]
    depth = N2
    rows = bins // depth
    whole_length = 2 * bins * devices
    own = N1 // devices
    span = N1 + 2 * DM
    half_tiles = -(-span // (2 * LANES))
    width = -(-own // LANES) * LANES + LANES
    tabs = tables(depth, rows, whole_length, half_tiles, devices)
    start, col_first, col_step, row_first, row_step, offset = (jnp.asarray(t) for t in tabs[:6])
    flip = jnp.asarray(tabs[6], jnp.bfloat16)
    count = temps * dets
    vmem = pl.BlockSpec(memory_space=pltpu.VMEM)
    smem = pl.BlockSpec(memory_space=pltpu.SMEM)
    shaped_s = strain.reshape(2, dets, rows, depth)
    shaped_h = templates.reshape(2, temps, rows, depth)
    parts = pl.pallas_call(
        functools.partial(series_kernel, temps, dets, own, devices, copies, half_tiles, 1),
        out_shape=jax.ShapeDtypeStruct((devices * copies, ROWS, width), jnp.bfloat16),
        in_specs=[smem] + [vmem] * 9,
        out_specs=vmem,
        scratch_shapes=[
            pltpu.VMEM((2 * count * rows, depth), jnp.bfloat16),
            pltpu.VMEM((2, depth, LANES), jnp.float32),
            pltpu.VMEM((2, rows, LANES), jnp.float32),
            pltpu.VMEM((ROWS, 2 * half_tiles * LANES), jnp.bfloat16),
        ],
        compiler_params=pltpu.CompilerParams(vmem_limit_bytes=40 << 20),
        name="series",
    )(lengths, shaped_s, shaped_h, start, col_first, col_step, row_first, row_step, offset, flip)
    received = lax.all_to_all(parts, ("filt", "sky"), split_axis=0, concat_axis=0, tiled=True)
    tile = 2 * LANES
    weights = pl.pallas_call(
        functools.partial(weight_kernel, dets),
        out_shape=jax.ShapeDtypeStruct((sky // tile, dets * LANES, 2 * tile), jnp.bfloat16),
        in_specs=[vmem] * 2,
        out_specs=vmem,
        compiler_params=pltpu.CompilerParams(vmem_limit_bytes=16 << 20),
        cost_estimate=pl.CostEstimate(flops=1 << 22, bytes_accessed=3 << 20, transcendentals=0),
        name="weights",
    )(delays, antenna)
    best = pl.pallas_call(
        functools.partial(sky_kernel, temps, dets, own, devices, copies),
        out_shape=jax.ShapeDtypeStruct((own, sky), jnp.float32),
        grid=(sky // tile,),
        in_specs=[vmem, pl.BlockSpec((1, dets * LANES, 2 * tile), lambda i: (i, 0, 0))],
        out_specs=pl.BlockSpec((own, tile), lambda i: (0, i)),
        scratch_shapes=[pltpu.VMEM((copies * temps * 2 * own, dets * LANES), jnp.bfloat16)],
        compiler_params=pltpu.CompilerParams(vmem_limit_bytes=24 << 20),
        name="sky",
    )(received, weights)
    return best[None]


def solution(mesh):
    in_specs = (
        P(None, "grp", "filt"),
        P(None, "sky", "filt"),
        P("sky"),
        P(None, None, "sky"),
        P(None, "sky"),
    )
    out_specs = P("grp", "filt", "sky")
    return jax.shard_map(body, mesh=mesh, in_specs=in_specs, out_specs=out_specs, check_vma=False)
```

time: 39.2 us -> 38.8 us (0.990)
  waiting for transfers between devices: 8.93 us -> 8.52 us
    pallas_call x1, Pallas kernels: 9.96 us -> 9.28 us  [body(): pl.pallas_call(functools.partial(sky_kernel, temps, dets, own, devices, c...]
    all_to_all x1, waiting for transfers between devices: 8.93 us -> 8.52 us  [body(): lax.all_to_all(parts, ('filt', 'sky'), split_axis=0, concat_axis=0, tiled...]
  transfers between devices with their start and end apart: 1 -> 1, of which waited for: 1 -> 1; matrix products, arithmetic and copies ran while one was open for 0% -> 0% of each run, Pallas kernels for 0% -> 1%
where the time goes in v1:
time: 38.8 us; the launch traced here: 38.5 us
  Pallas kernels  18.5 us (48%)
  waiting for transfers between devices  8.52 us (22%)
  starting transfers between devices  7.43 us (19%)
  local copies, waits for them, and re-layouts  3.93 us (10%)
    pallas_call x1, Pallas kernels, body(): pl.pallas_call(functools.partial(sky_kernel, temps, dets, own, devices, c...  9.28 us
    pallas_call x1, Pallas kernels, body(): pl.pallas_call(functools.partial(series_kernel, temps, dets, own, devices...  8.79 us
    all_to_all x1, waiting for transfers between devices, body(): lax.all_to_all(parts, ('filt', 'sky'), split_axis=0, concat_axis=0, tiled...  8.52 us
    all_to_all x1, starting transfers between devices, body(): lax.all_to_all(parts, ('filt', 'sky'), split_axis=0, concat_axis=0, tiled...  7.43 us
    reshape x2, local copies, waits for them, and re-layouts, body(): shaped_s = strain.reshape(2, dets, rows, depth)  2.37 us
    reshape x1, local copies, waits for them, and re-layouts, body(): shaped_h = templates.reshape(2, temps, rows, depth)  1.5 us
  transfers between devices with their start and end apart: 1, of which 1 were waited for; matrix products, arithmetic and copies ran while one was open for 0% of the time, Pallas kernels for 1%

profile of v1, /device:TPU:0, one launch (start us, length us, event | category | flops | bytes accessed | tf_op | source)
XLA Modules:
  0.0 38.5 jit_solution(15822145320364655226)
XLA Ops:
  0.0 0.0 copy-start.5
  0.0 0.0 copy-start.1
  0.0 0.0 copy-start.2
  0.0 0.0 copy-start.8
  0.1 1.5 %reshape.7.templates = bf16[2,2,128,512]{3,2,1,0:T(8,128)(2,1)S(1)} reshape(bf16[2,2,65536]{2,1,0:T(2,128)(2,1)} %param.13) | data formatting | bytes 1048576 | tf_op jit(solution)/shard_map/reshape | solution.py:247
  1.6 2.3 %reshape.6 = bf16[2,3,128,512]{3,2,0,1:T(8,128)(2,1)S(1)} reshape(bf16[2,3,65536]{2,0,1:T(2,128)(2,1)} %param.12) | data formatting | bytes 1572864 | tf_op jit(solution)/shard_map/reshape | solution.py:246
  3.9 0.0 copy-start.9
  3.9 0.0 copy-start.6
  3.9 0.1 copy.15.strain
  4.0 0.0 copy-done.5
  4.0 0.0 copy-done.7
  4.0 0.0 copy-done.3
  4.0 0.0 copy-done.4
  4.0 0.0 copy-done
  4.0 0.0 copy-done.1
  4.0 0.0 copy-done.2
  4.0 0.0 copy-done.8
  4.1 8.8 %series.1 = bf16[16,16,384]{2,1,0:T(8,128)(2,1)} custom-call(s32[2]{0:T(128)S(1)} %copy-done.8, bf16[2,3,128,512]{3,2,1,0:T(8,128)(2,1)S(1)} %copy.15.strain, bf16[2,2,128,512]{3,2,1,0:T(8,128)(2,1)S(1)} %reshape.7.templates, f32[2,128,512]{2,1,0:T(8,128)S(1)} %copy-done.2, f32[2,512,128]{2,1,0:T(8,128)S(1)} %copy-done.1, f32[2,512,128]{2,1,0:T(8,128)S(1)} %copy-done, ...), custom_call_target="tpu_custom_call" | custom-call | tf_op jit(solution)/shard_map/series/pallas_call | solution.py:248
  12.8 7.4 %all-to-all-start = ((bf16[16,16,384]{2,1,0:T(8,128)(2,1)}), bf16[16,16,384]{2,1,0:T(8,128)(2,1)S(1)}, u32[]{:S(2)}, u32[]{:S(2)}) async-start(bf16[16,16,384]{2,1,0:T(8,128)(2,1)} %series.1), calls=%async_computation | async-start | bytes 393216 | tf_op jit(solution)/shard_map/all_to_all | solution.py:262
  20.3 0.0 copy-done.9
  20.3 0.0 copy-done.6
  20.3 0.4 %weights.1 = bf16[6,384,512]{2,1,0:T(8,128)(2,1)S(1)} custom-call(s32[3,1536]{1,0:T(4,128)S(1)} %copy-done.6, bf16[2,3,1536]{2,1,0:T(4,128)(2,1)S(1)} %copy.16.antenna), custom_call_target="tpu_custom_call" | custom-call | flops 4194304 | bytes 3145728 | tf_op jit(solution)/shard_map/weights/pallas_call | solution.py:264
  20.7 8.5 %all-to-all-done.received = bf16[16,16,384]{2,1,0:T(8,128)(2,1)S(1)} async-done(((bf16[16,16,384]{2,1,0:T(8,128)(2,1)}), bf16[16,16,384]{2,1,0:T(8,128)(2,1)S(1)}, u32[]{:S(2)}, u32[]{:S(2)}) %all-to-all-start) | async-done | bytes 196640 | tf_op jit(solution)/shard_map/all_to_all | solution.py:262
  29.2 9.3 %sky.1 = f32[256,1536]{1,0:T(8,128)} custom-call(bf16[16,16,384]{2,1,0:T(8,128)(2,1)S(1)} %all-to-all-done.received, bf16[6,384,512]{2,1,0:T(8,128)(2,1)S(1)} %weights.1), custom_call_target="tpu_custom_call" | custom-call | tf_op jit(solution)/shard_map/sky/pallas_call | solution.py:273
  (5 shorter events, 0.0 us)
Async XLA Ops:
  0.0 4.0 %copy-start.5 = (bf16[128,128]{1,0:T(8,128)(2,1)S(1)}, bf16[128,128]{1,0:T(8,128)(2,1)}, u32[]{:S(2)}) copy-start(bf16[128,128]{1,0:T(8,128)(2,1)} %constant.20.clone.flip) | copy-start | bytes 98308
  0.0 4.0 %copy-start.7 = (f32[8,4,128]{2,1,0:T(4,128)S(1)}, f32[8,4,128]{2,1,0:T(4,128)}, u32[]{:S(2)}) copy-start(f32[8,4,128]{2,1,0:T(4,128)} %constant.19.clone.offset) | copy-start | bytes 49156
  0.0 4.0 %copy-start.3 = (f32[2,128,128]{2,1,0:T(8,128)S(1)}, f32[2,128,128]{2,1,0:T(8,128)}, u32[]{:S(2)}) copy-start(f32[2,128,128]{2,1,0:T(8,128)} %constant.18.clone.row_step) | copy-start | bytes 393220
  0.0 4.0 %copy-start.4 = (f32[2,128,128]{2,1,0:T(8,128)S(1)}, f32[2,128,128]{2,1,0:T(8,128)}, u32[]{:S(2)}) copy-start(f32[2,128,128]{2,1,0:T(8,128)} %constant.17.clone.row_first) | copy-start | bytes 393220
  0.0 4.0 %copy-start = (f32[2,512,128]{2,1,0:T(8,128)S(1)}, f32[2,512,128]{2,1,0:T(8,128)}, u32[]{:S(2)}) copy-start(f32[2,512,128]{2,1,0:T(8,128)} %constant.16.clone.col_step) | copy-start | bytes 1572868
  0.0 4.0 %copy-start.1 = (f32[2,512,128]{2,1,0:T(8,128)S(1)}, f32[2,512,128]{2,1,0:T(8,128)}, u32[]{:S(2)}) copy-start(f32[2,512,128]{2,1,0:T(8,128)} %constant.15.clone.col_first) | copy-start | bytes 1572868
  0.0 4.0 %copy-start.2 = (f32[2,128,512]{2,1,0:T(8,128)S(1)}, f32[2,128,512]{2,1,0:T(8,128)}, u32[]{:S(2)}) copy-start(f32[2,128,512]{2,1,0:T(8,128)} %constant.14.clone.start) | copy-start | bytes 1572868
  0.0 4.0 %copy-start.8 = (s32[2]{0:T(128)S(1)}, s32[2]{0:T(128)}, u32[]{:S(2)}) copy-start(s32[2]{0:T(128)} %lengths.1) | copy-start | bytes 28
  3.9 16.4 %copy-start.9 = (bf16[2,3,1536]{2,0,1:T(2,128)(2,1)S(1)}, bf16[2,3,1536]{2,0,1:T(2,128)(2,1)}, u32[]{:S(2)}) copy-start(bf16[2,3,1536]{2,0,1:T(2,128)(2,1)} %param.15) | copy-start | bytes 55300
  3.9 16.4 %copy-start.6 = (s32[3,1536]{1,0:T(4,128)S(1)}, s32[3,1536]{1,0:T(4,128)}, u32[]{:S(2)}) copy-start(s32[3,1536]{1,0:T(4,128)} %delays.1) | copy-start | bytes 55300
  12.8 16.4 %all-to-all-start = ((bf16[16,16,384]{2,1,0:T(8,128)(2,1)}), bf16[16,16,384]{2,1,0:T(8,128)(2,1)S(1)}, u32[]{:S(2)}, u32[]{:S(2)}) async-start(bf16[16,16,384]{2,1,0:T(8,128)(2,1)} %series.1), calls=%async_computation | async-start | bytes 393216 | tf_op jit(solution)/shard_map/all_to_all | solution.py:262

commit v2 on v1

--- a/solution.py
+++ b/solution.py
@@ -156,22 +156,31 @@
             out[target * copies + copy] = window
 
 
-def weight_kernel(dets, delays, antenna, weights):
-    tile = 2 * LANES
+def weight_kernel(dets, tile, delays, antenna, weights):
     sky = delays.shape[1]
     lag = DM - lax.broadcasted_iota(jnp.int32, (LANES, tile), 0)
     for i in range(sky // tile):
         part = slice(i * tile, (i + 1) * tile)
+        rows = [[antenna[p, d : d + 1, part].astype(jnp.float32) for d in range(dets)] for p in range(2)]
+        x, y = rows[0][-1], rows[1][-1]
+        most = jnp.maximum(jnp.abs(x), jnp.abs(y))
+        some = most > 0.0
+        least = jnp.where(some, most, 1.0)
+        x, y = jnp.where(some, x / least, 1.0), jnp.where(some, y / least, 0.0)
+        unit = lax.rsqrt(x * x + y * y)
+        cos, sin = x * unit, y * unit
+        first = [cos * rows[0][d] + sin * rows[1][d] for d in range(dets)]
+        second = [cos * rows[1][d] - sin * rows[0][d] for d in range(dets - 1)]
         for d in range(dets):
             hit = lag == delays[d : d + 1, part]
-            for p in range(2):
-                value = jnp.where(hit, antenna[p, d : d + 1, part].astype(jnp.float32), 0.0)
-                weights[i, d * LANES : (d + 1) * LANES, p * tile : (p + 1) * tile] = value.astype(jnp.bfloat16)
+            weights[i, d * LANES : (d + 1) * LANES, :] = jnp.where(hit, first[d], 0.0).astype(jnp.bfloat16)
+            if d < dets - 1:
+                place = (dets + d) * LANES
+                weights[i, place : place + LANES, :] = jnp.where(hit, second[d], 0.0).astype(jnp.bfloat16)
 
 
 def sky_kernel(temps, dets, own, sources, copies, received, weights, out, hankel):
     width = received.shape[2]
-    tile = 2 * LANES
     count = temps * dets
     blocks = -(-own // LANES)
     groups = 2 * copies * temps
@@ -212,15 +221,19 @@
     span = min(128, own)
     for first in range(0, own, ROWS):
         if first % span == 0:
-            mixed = jnp.dot(
-                hankel[first * groups : (first + span) * groups, :], weights[0], preferred_element_type=jnp.float32
+            here = slice(first * groups, (first + span) * groups)
+            lags = dets * LANES
+            mixed_a = jnp.dot(hankel[here, :], weights[0, :lags, :], preferred_element_type=jnp.float32)
+            mixed_b = jnp.dot(
+                hankel[here, : lags - LANES], weights[0, lags:, :], preferred_element_type=jnp.float32
             )
         best = None
         for k in range(copies * temps):
             place = first % span * groups + 2 * k * ROWS
-            re, im = mixed[place : place + ROWS], mixed[place + ROWS : place + 2 * ROWS]
-            power = re * re + im * im
-            power = power[:, :tile] + power[:, tile:]
+            power = None
+            for mixed in (mixed_a, mixed_b):
+                for part in (mixed[place : place + ROWS], mixed[place + ROWS : place + 2 * ROWS]):
+                    power = part * part if power is None else power + part * part
             best = power if best is None else jnp.maximum(best, power)
         out[first : first + ROWS, :] = best
 
@@ -260,10 +273,10 @@
         name="series",
     )(lengths, shaped_s, shaped_h, start, col_first, col_step, row_first, row_step, offset, flip)
     received = lax.all_to_all(parts, ("filt", "sky"), split_axis=0, concat_axis=0, tiled=True)
-    tile = 2 * LANES
+    tile = 4 * LANES if sky % (4 * LANES) == 0 else 2 * LANES
     weights = pl.pallas_call(
-        functools.partial(weight_kernel, dets),
-        out_shape=jax.ShapeDtypeStruct((sky // tile, dets * LANES, 2 * tile), jnp.bfloat16),
+        functools.partial(weight_kernel, dets, tile),
+        out_shape=jax.ShapeDtypeStruct((sky // tile, (2 * dets - 1) * LANES, tile), jnp.bfloat16),
         in_specs=[vmem] * 2,
         out_specs=vmem,
         compiler_params=pltpu.CompilerParams(vmem_limit_bytes=16 << 20),
@@ -274,7 +287,7 @@
         functools.partial(sky_kernel, temps, dets, own, devices, copies),
         out_shape=jax.ShapeDtypeStruct((own, sky), jnp.float32),
         grid=(sky // tile,),
-        in_specs=[vmem, pl.BlockSpec((1, dets * LANES, 2 * tile), lambda i: (i, 0, 0))],
+        in_specs=[vmem, pl.BlockSpec((1, (2 * dets - 1) * LANES, tile), lambda i: (i, 0, 0))],
         out_specs=pl.BlockSpec((own, tile), lambda i: (0, i)),
         scratch_shapes=[pltpu.VMEM((copies * temps * 2 * own, dets * LANES), jnp.bfloat16)],
         compiler_params=pltpu.CompilerParams(vmem_limit_bytes=24 << 20),

time: 38.8 us -> 36.8 us (0.948)
  Pallas kernels: 18.5 us -> 16.5 us
    pallas_call x1, Pallas kernels: 9.28 us -> 7.22 us  [body(): pl.pallas_call(functools.partial(sky_kernel, temps, dets, own, devices, c...]
where the time goes in v2:
time: 36.8 us; the launch traced here: 36.5 us
  Pallas kernels  16.5 us (45%)
  waiting for transfers between devices  8.47 us (23%)
  starting transfers between devices  7.43 us (20%)
  local copies, waits for them, and re-layouts  3.95 us (11%)
    pallas_call x1, Pallas kernels, body(): pl.pallas_call(functools.partial(series_kernel, temps, dets, own, devices...  8.81 us
    all_to_all x1, waiting for transfers between devices, body(): lax.all_to_all(parts, ('filt', 'sky'), split_axis=0, concat_axis=0, tiled...  8.47 us
    all_to_all x1, starting transfers between devices, body(): lax.all_to_all(parts, ('filt', 'sky'), split_axis=0, concat_axis=0, tiled...  7.43 us
    pallas_call x1, Pallas kernels, body(): pl.pallas_call(functools.partial(sky_kernel, temps, dets, own, devices, c...  7.22 us
    reshape x2, local copies, waits for them, and re-layouts, body(): shaped_s = strain.reshape(2, dets, rows, depth)  2.39 us
    reshape x1, local copies, waits for them, and re-layouts, body(): shaped_h = templates.reshape(2, temps, rows, depth)  1.5 us
  transfers between devices with their start and end apart: 1, of which 1 were waited for; matrix products, arithmetic and copies ran while one was open for 0% of the time, Pallas kernels for 1%

profile of v2, /device:TPU:0, one launch (start us, length us, event | category | flops | bytes accessed | tf_op | source)
XLA Modules:
  0.0 36.5 jit_solution(16614543846815279396)
XLA Ops:
  0.0 0.0 copy-start
  0.0 0.0 copy-start.5
  0.0 0.0 copy-start.7
  0.0 0.0 copy-start.8
  0.1 1.5 %reshape.7.templates = bf16[2,2,128,512]{3,2,1,0:T(8,128)(2,1)S(1)} reshape(bf16[2,2,65536]{2,1,0:T(2,128)(2,1)} %param.13) | data formatting | bytes 1048576 | tf_op jit(solution)/shard_map/reshape | solution.py:260
  1.6 2.3 %reshape.6 = bf16[2,3,128,512]{3,2,0,1:T(8,128)(2,1)S(1)} reshape(bf16[2,3,65536]{2,0,1:T(2,128)(2,1)} %param.12) | data formatting | bytes 1572864 | tf_op jit(solution)/shard_map/reshape | solution.py:259
  3.9 0.1 copy.15.strain
  4.0 0.0 copy-done
  4.0 0.0 copy-done.1
  4.0 0.0 copy-done.2
  4.0 0.0 copy-done.3
  4.0 0.0 copy-done.4
  4.0 0.0 copy-done.5
  4.0 0.0 copy-done.7
  4.0 0.0 copy-done.8
  4.0 0.0 copy-start.9
  4.1 0.0 copy-start.6
  4.1 8.8 %series.1 = bf16[16,16,384]{2,1,0:T(8,128)(2,1)} custom-call(s32[2]{0:T(128)S(1)} %copy-done.8, bf16[2,3,128,512]{3,2,1,0:T(8,128)(2,1)S(1)} %copy.15.strain, bf16[2,2,128,512]{3,2,1,0:T(8,128)(2,1)S(1)} %reshape.7.templates, f32[2,128,512]{2,1,0:T(8,128)S(1)} %copy-done.2, f32[2,512,128]{2,1,0:T(8,128)S(1)} %copy-done.1, f32[2,512,128]{2,1,0:T(8,128)S(1)} %copy-done, ...), custom_call_target="tpu_custom_call" | custom-call | tf_op jit(solution)/shard_map/series/pallas_call | solution.py:261
  12.9 7.4 %all-to-all-start = ((bf16[16,16,384]{2,1,0:T(8,128)(2,1)}), bf16[16,16,384]{2,1,0:T(8,128)(2,1)S(1)}, u32[]{:S(2)}, u32[]{:S(2)}) async-start(bf16[16,16,384]{2,1,0:T(8,128)(2,1)} %series.1), calls=%async_computation | async-start | bytes 393216 | tf_op jit(solution)/shard_map/all_to_all | solution.py:275
  20.3 0.0 copy-done.9
  20.3 0.0 copy-done.6
  20.3 0.4 %weights.1 = bf16[3,640,512]{2,1,0:T(8,128)(2,1)S(1)} custom-call(s32[3,1536]{1,0:T(4,128)S(1)} %copy-done.6, bf16[2,3,1536]{2,1,0:T(4,128)(2,1)S(1)} %copy.16.antenna), custom_call_target="tpu_custom_call" | custom-call | flops 4194304 | bytes 3145728 | tf_op jit(solution)/shard_map/weights/pallas_call | solution.py:277
  20.8 8.5 %all-to-all-done.received = bf16[16,16,384]{2,1,0:T(8,128)(2,1)S(1)} async-done(((bf16[16,16,384]{2,1,0:T(8,128)(2,1)}), bf16[16,16,384]{2,1,0:T(8,128)(2,1)S(1)}, u32[]{:S(2)}, u32[]{:S(2)}) %all-to-all-start) | async-done | bytes 196640 | tf_op jit(solution)/shard_map/all_to_all | solution.py:275
  29.3 7.2 %sky.1 = f32[256,1536]{1,0:T(8,128)} custom-call(bf16[16,16,384]{2,1,0:T(8,128)(2,1)S(1)} %all-to-all-done.received, bf16[3,640,512]{2,1,0:T(8,128)(2,1)S(1)} %weights.1), custom_call_target="tpu_custom_call" | custom-call | tf_op jit(solution)/shard_map/sky/pallas_call | solution.py:286
  (5 shorter events, 0.0 us)
Async XLA Ops:
  0.0 4.0 %copy-start = (f32[2,512,128]{2,1,0:T(8,128)S(1)}, f32[2,512,128]{2,1,0:T(8,128)}, u32[]{:S(2)}) copy-start(f32[2,512,128]{2,1,0:T(8,128)} %constant.16.clone.col_step) | copy-start | bytes 1572868
  0.0 4.0 %copy-start.1 = (f32[2,512,128]{2,1,0:T(8,128)S(1)}, f32[2,512,128]{2,1,0:T(8,128)}, u32[]{:S(2)}) copy-start(f32[2,512,128]{2,1,0:T(8,128)} %constant.15.clone.col_first) | copy-start | bytes 1572868
  0.0 4.0 %copy-start.2 = (f32[2,128,512]{2,1,0:T(8,128)S(1)}, f32[2,128,512]{2,1,0:T(8,128)}, u32[]{:S(2)}) copy-start(f32[2,128,512]{2,1,0:T(8,128)} %constant.14.clone.start) | copy-start | bytes 1572868
  0.0 4.0 %copy-start.3 = (f32[2,128,128]{2,1,0:T(8,128)S(1)}, f32[2,128,128]{2,1,0:T(8,128)}, u32[]{:S(2)}) copy-start(f32[2,128,128]{2,1,0:T(8,128)} %constant.18.clone.row_step) | copy-start | bytes 393220
  0.0 4.0 %copy-start.4 = (f32[2,128,128]{2,1,0:T(8,128)S(1)}, f32[2,128,128]{2,1,0:T(8,128)}, u32[]{:S(2)}) copy-start(f32[2,128,128]{2,1,0:T(8,128)} %constant.17.clone.row_first) | copy-start | bytes 393220
  0.0 4.0 %copy-start.5 = (bf16[128,128]{1,0:T(8,128)(2,1)S(1)}, bf16[128,128]{1,0:T(8,128)(2,1)}, u32[]{:S(2)}) copy-start(bf16[128,128]{1,0:T(8,128)(2,1)} %constant.20.clone.flip) | copy-start | bytes 98308
  0.0 4.0 %copy-start.7 = (f32[8,4,128]{2,1,0:T(4,128)S(1)}, f32[8,4,128]{2,1,0:T(4,128)}, u32[]{:S(2)}) copy-start(f32[8,4,128]{2,1,0:T(4,128)} %constant.19.clone.offset) | copy-start | bytes 49156
  0.0 4.0 %copy-start.8 = (s32[2]{0:T(128)S(1)}, s32[2]{0:T(128)}, u32[]{:S(2)}) copy-start(s32[2]{0:T(128)} %lengths.1) | copy-start | bytes 28
  4.0 16.3 %copy-start.9 = (bf16[2,3,1536]{2,0,1:T(2,128)(2,1)S(1)}, bf16[2,3,1536]{2,0,1:T(2,128)(2,1)}, u32[]{:S(2)}) copy-start(bf16[2,3,1536]{2,0,1:T(2,128)(2,1)} %param.15) | copy-start | bytes 55300
  4.1 16.3 %copy-start.6 = (s32[3,1536]{1,0:T(4,128)S(1)}, s32[3,1536]{1,0:T(4,128)}, u32[]{:S(2)}) copy-start(s32[3,1536]{1,0:T(4,128)} %delays.1) | copy-start | bytes 55300
  12.9 16.4 %all-to-all-start = ((bf16[16,16,384]{2,1,0:T(8,128)(2,1)}), bf16[16,16,384]{2,1,0:T(8,128)(2,1)S(1)}, u32[]{:S(2)}, u32[]{:S(2)}) async-start(bf16[16,16,384]{2,1,0:T(8,128)(2,1)} %series.1), calls=%async_computation | async-start | bytes 393216 | tf_op jit(solution)/shard_map/all_to_all | solution.py:275

commit v3 on v2

--- a/solution.py
+++ b/solution.py
@@ -25,13 +25,18 @@
     centre2 = 2 * (2 * N1 + DM) - 2 * half_tiles * LANES - 1
     row = np.arange(rows, dtype=np.int64)[:, None]
     col = np.arange(depth, dtype=np.int64)[None, :]
-    odd = 2 * np.arange(LANES, dtype=np.int64)[None, :] + 1
-    turns = 2 * whole_length
-    start = turn(((row * depth + col) * centre2 % turns) / turns)
-    col_first = turn((col.T * odd % turns) / turns)
-    col_step = turn((col.T * (2 * LANES) % turns) / turns * np.ones((1, LANES)))
-    row_first = turn((row * depth * odd % turns) / turns)
-    row_step = turn((row * depth * (2 * LANES) % turns) / turns * np.ones((1, LANES)))
+    odd = 2 * np.arange(2 * LANES, dtype=np.int64)[None, :] + 1
+    pair = 2 * np.arange(depth // 2, dtype=np.int64)[:, None] + 1
+    middle = 2 * row * depth + depth - 1
+    step = 4 * LANES * np.ones((1, 2 * LANES), np.int64)
+    turns = 4 * whole_length
+    start = turn(((row * depth + col) * (2 * centre2) % turns) / turns)
+    start = np.concatenate([start[:, :, depth // 2 :], start[:, :, : depth // 2][:, :, ::-1]])
+    col_first = turn((pair * odd % turns) / turns)
+    col_step = turn((pair * step % turns) / turns)
+    row_first = turn((middle * odd % turns) / turns)
+    row_step = turn((middle * step % turns) / turns)
+    odd = odd[:, :LANES]
     pos = np.arange(devices, dtype=np.int64)[:, None]
     t_up = (centre2 + odd) // 2
     t_down = (centre2 - odd) // 2
@@ -39,84 +44,99 @@
     up = turn((pos * base * t_up % whole_length) / whole_length)
     down = turn((pos * base * t_down % whole_length) / whole_length)
     offset = np.concatenate([up, down]).transpose(1, 0, 2)
-    flip = np.eye(LANES, dtype=np.float32)[::-1]
+    flip = np.eye(2 * LANES, dtype=np.float32)[::-1]
     return start, col_first, col_step, row_first, row_step, offset, flip
 
 
 def series_kernel(
-    temps, dets, own, devices, copies, half_tiles, together,
+    temps, dets, own, devices, copies, half_tiles,
     lengths, strain, templates, start, col_first, col_step, row_first, row_step, offset, flip,
-    out, spectra, col_now, row_now, series,
+    out, even, odd, back_s, back_h, col_now, row_now, series,
 ):
     rows, depth = strain.shape[2], strain.shape[3]
+    side = depth // 2
     count = temps * dets
     pos = lax.axis_index("filt")
-    norms = [jnp.zeros((ROWS, depth), jnp.float32) for _ in range(temps)]
+    for r in range(2):
+        for d in range(dets):
+            turned = jnp.dot(strain[r, d, :, :side], flip[...], preferred_element_type=jnp.float32)
+            back_s[r, d] = turned.astype(jnp.bfloat16)
+        for k in range(temps):
+            turned = jnp.dot(templates[r, k, :, :side], flip[...], preferred_element_type=jnp.float32)
+            back_h[r, k] = turned.astype(jnp.bfloat16)
+    norms = [jnp.zeros((ROWS, side), jnp.float32) for _ in range(temps)]
 
     def filter_chunk(step, norms):
         first = pl.multiple_of(step * ROWS, ROWS)
         here = pl.ds(first, ROWS)
-        bins = (
-            (pos * rows + first) * depth
-            + lax.broadcasted_iota(jnp.int32, (ROWS, depth), 0) * depth
-            + lax.broadcasted_iota(jnp.int32, (ROWS, depth), 1)
-        )
-        s_re = [strain[0, d, here, :].astype(jnp.float32) for d in range(dets)]
-        s_im = [strain[1, d, here, :].astype(jnp.float32) for d in range(dets)]
-        p_re, p_im = start[0, here, :], start[1, here, :]
+        row_bin = (pos * rows + first) * depth + lax.broadcasted_iota(jnp.int32, (ROWS, side), 0) * depth
+        lane = lax.broadcasted_iota(jnp.int32, (ROWS, side), 1)
+        bins = (row_bin + side + lane, row_bin + side - 1 - lane)
+        s_re = [(strain[0, d, here, side:].astype(jnp.float32), back_s[0, d, here, :].astype(jnp.float32)) for d in range(dets)]
+        s_im = [(strain[1, d, here, side:].astype(jnp.float32), back_s[1, d, here, :].astype(jnp.float32)) for d in range(dets)]
         added = []
         for k in range(temps):
-            inside = bins < lengths[k]
-            h_re = jnp.where(inside, templates[0, k, here, :].astype(jnp.float32), 0.0)
-            h_im = jnp.where(inside, templates[1, k, here, :].astype(jnp.float32), 0.0)
-            added.append(norms[k] + (h_re * h_re + h_im * h_im))
-            g_re = h_re * p_re + h_im * p_im
-            g_im = h_re * p_im - h_im * p_re
+            energy = norms[k]
+            h_all = (
+                (templates[0, k, here, side:], templates[1, k, here, side:]),
+                (back_h[0, k, here, :], back_h[1, k, here, :]),
+            )
+            g = []
+            for i in range(2):
+                inside = bins[i] < lengths[k]
+                h_re = jnp.where(inside, h_all[i][0].astype(jnp.float32), 0.0)
+                h_im = jnp.where(inside, h_all[i][1].astype(jnp.float32), 0.0)
+                energy = energy + (h_re * h_re + h_im * h_im)
+                p_re, p_im = start[2 * i, here, :], start[2 * i + 1, here, :]
+                g.append((h_re * p_re + h_im * p_im, h_re * p_im - h_im * p_re))
+            added.append(energy)
             for d in range(dets):
                 place = 2 * ((k * dets + d) * rows + first)
-                x_re = g_re * s_re[d] - g_im * s_im[d]
-                x_im = g_re * s_im[d] + g_im * s_re[d]
-                spectra[pl.ds(pl.multiple_of(place, ROWS), ROWS), :] = x_re.astype(jnp.bfloat16)
-                spectra[pl.ds(pl.multiple_of(place + ROWS, ROWS), ROWS), :] = x_im.astype(jnp.bfloat16)
+                x_re = [g[i][0] * s_re[d][i] - g[i][1] * s_im[d][i] for i in range(2)]
+                x_im = [g[i][0] * s_im[d][i] + g[i][1] * s_re[d][i] for i in range(2)]
+                at_re = pl.ds(pl.multiple_of(place, ROWS), ROWS)
+                at_im = pl.ds(pl.multiple_of(place + ROWS, ROWS), ROWS)
+                even[at_re, :] = (x_re[0] + x_re[1]).astype(jnp.bfloat16)
+                even[at_im, :] = (x_im[0] + x_im[1]).astype(jnp.bfloat16)
+                odd[at_re, :] = (x_re[0] - x_re[1]).astype(jnp.bfloat16)
+                odd[at_im, :] = (x_im[0] - x_im[1]).astype(jnp.bfloat16)
         return added
 
     norms = lax.fori_loop(0, rows // ROWS, filter_chunk, norms)
-    high, low = [], []
-    for k in range(temps):
-        total = jnp.sum(jnp.sum(norms[k], axis=0, keepdims=True), axis=1, keepdims=True)
-        total = jnp.broadcast_to(total, (1, LANES))
-        first = total.astype(jnp.bfloat16).astype(jnp.float32)
-        high.append(first)
-        low.append(total - first)
-    f_ur, f_ui, f_dr, f_di = (offset[pos, i : i + 1, :] for i in range(4))
-
     col_now[...] = col_first[...]
     row_now[...] = row_first[...]
 
-    def section(tile):
+    def section(tile, tiles, last):
+        wide = tiles * LANES
+        high, low = [], []
+        for k in range(temps):
+            total = jnp.sum(jnp.sum(norms[k], axis=0, keepdims=True), axis=1, keepdims=True)
+            total = jnp.broadcast_to(total, (1, wide))
+            first = total.astype(jnp.bfloat16).astype(jnp.float32)
+            high.append(first)
+            low.append(total - first)
+        f_ur, f_ui, f_dr, f_di = (
+            jnp.concatenate([offset[pos, i : i + 1, :]] * tiles, axis=1) for i in range(4)
+        )
         c_re, c_im = col_now[0], col_now[1]
-        table = jnp.concatenate([c_re, c_im], axis=1).astype(jnp.bfloat16)
-        d_re, d_im = col_step[0], col_step[1]
-        col_now[0] = c_re * d_re - c_im * d_im
-        col_now[1] = c_re * d_im + c_im * d_re
-        parts = 2
-        height = spectra.shape[0] // parts
-        pieces = [
-            jnp.dot(spectra[i * height : (i + 1) * height, :], table, preferred_element_type=jnp.float32)
-            for i in range(parts)
-        ]
+        cos, sin = c_re[:, :wide].astype(jnp.bfloat16), c_im[:, :wide].astype(jnp.bfloat16)
+        if not last:
+            d_re, d_im = col_step[0], col_step[1]
+            col_now[0] = c_re * d_re - c_im * d_im
+            col_now[1] = c_re * d_im + c_im * d_re
+        on_even = jnp.dot(even[...], cos, preferred_element_type=jnp.float32)
+        on_odd = jnp.dot(odd[...], sin, preferred_element_type=jnp.float32)
         up_re, up_im, down_re, down_im = [], [], [], []
         for q in range(count):
             s1 = s2 = s3 = s4 = None
             for block in range(0, rows, ROWS):
-                place = 2 * (q * rows + block)
                 for half in range(0, ROWS, 8):
-                    w_re = row_now[0, block + half : block + half + 8, :]
-                    w_im = row_now[1, block + half : block + half + 8, :]
-                    sums = pieces[place // height]
-                    top, end = place % height + half, place % height + ROWS + half
-                    a, d = sums[top : top + 8, :LANES], sums[top : top + 8, LANES:]
-                    e, b = sums[end : end + 8, :LANES], sums[end : end + 8, LANES:]
+                    w_re = row_now[0, block + half : block + half + 8, :wide]
+                    w_im = row_now[1, block + half : block + half + 8, :wide]
+                    top = 2 * (q * rows + block) + half
+                    end = top + ROWS
+                    a, e = on_even[top : top + 8], on_even[end : end + 8]
+                    d, b = on_odd[top : top + 8], on_odd[end : end + 8]
                     n1, n2 = a * w_re - d * w_im, b * w_re + e * w_im
                     n3, n4 = e * w_re - b * w_im, d * w_re + a * w_im
                     s1 = n1 if s1 is None else s1 + n1
@@ -133,20 +153,23 @@
             down_im.append(r * f_di + i * f_dr)
         upper = jnp.concatenate(up_re + high + up_im + low, axis=0).astype(jnp.bfloat16)
         lower = jnp.concatenate(down_re + high + down_im + low, axis=0).astype(jnp.bfloat16)
-        upper = jnp.dot(upper, flip[...], preferred_element_type=jnp.float32).astype(jnp.bfloat16)
-        series[:, pl.ds(pl.multiple_of((half_tiles - 1 - tile) * LANES, LANES), LANES)] = upper
-        series[:, pl.ds(pl.multiple_of((half_tiles + tile) * LANES, LANES), LANES)] = lower
-        w_re, w_im = row_now[0], row_now[1]
-        d_re, d_im = row_step[0], row_step[1]
-        row_now[0] = w_re * d_re - w_im * d_im
-        row_now[1] = w_re * d_im + w_im * d_re
+        turned = flip[2 * LANES - wide :, :wide]
+        upper = jnp.dot(upper, turned, preferred_element_type=jnp.float32).astype(jnp.bfloat16)
+        series[:, pl.ds(pl.multiple_of((half_tiles - tiles - tile) * LANES, LANES), wide)] = upper
+        series[:, pl.ds(pl.multiple_of((half_tiles + tile) * LANES, LANES), wide)] = lower
+        if not last:
+            w_re, w_im = row_now[0], row_now[1]
+            d_re, d_im = row_step[0], row_step[1]
+            row_now[0] = w_re * d_re - w_im * d_im
+            row_now[1] = w_re * d_im + w_im * d_re
 
     def some(step, carry):
-        for sub in range(together):
-            section(step * together + sub)
+        section(2 * step, 2, False)
         return carry
 
-    lax.fori_loop(0, half_tiles // together, some, 0)
+    lax.fori_loop(0, half_tiles // 2, some, 0)
+    if half_tiles % 2:
+        section(half_tiles - 1, 1, True)
 
     width = out.shape[2]
     for target in range(devices):
@@ -243,7 +266,7 @@
     copies = lax.axis_size("sky")
     temps, dets, bins = templates.shape[1], strain.shape[1], strain.shape[2]
     sky = delays.shape[1]
-    depth = N2
+    depth = 4 * LANES
     rows = bins // depth
     whole_length = 2 * bins * devices
     own = N1 // devices
@@ -259,14 +282,17 @@
     shaped_s = strain.reshape(2, dets, rows, depth)
     shaped_h = templates.reshape(2, temps, rows, depth)
     parts = pl.pallas_call(
-        functools.partial(series_kernel, temps, dets, own, devices, copies, half_tiles, 1),
+        functools.partial(series_kernel, temps, dets, own, devices, copies, half_tiles),
         out_shape=jax.ShapeDtypeStruct((devices * copies, ROWS, width), jnp.bfloat16),
         in_specs=[smem] + [vmem] * 9,
         out_specs=vmem,
         scratch_shapes=[
-            pltpu.VMEM((2 * count * rows, depth), jnp.bfloat16),
-            pltpu.VMEM((2, depth, LANES), jnp.float32),
-            pltpu.VMEM((2, rows, LANES), jnp.float32),
+            pltpu.VMEM((2 * count * rows, depth // 2), jnp.bfloat16),
+            pltpu.VMEM((2 * count * rows, depth // 2), jnp.bfloat16),
+            pltpu.VMEM((2, dets, rows, depth // 2), jnp.bfloat16),
+            pltpu.VMEM((2, temps, rows, depth // 2), jnp.bfloat16),
+            pltpu.VMEM((2, depth // 2, 2 * LANES), jnp.float32),
+            pltpu.VMEM((2, rows, 2 * LANES), jnp.float32),
             pltpu.VMEM((ROWS, 2 * half_tiles * LANES), jnp.bfloat16),
         ],
         compiler_params=pltpu.CompilerParams(vmem_limit_bytes=40 << 20),

time: 36.8 us -> 36.4 us (0.989)
  Pallas kernels: 16.5 us -> 14.1 us
  local copies, waits for them, and re-layouts: 3.95 us -> 5.89 us
    pallas_call x1, Pallas kernels: 8.81 us -> 6.45 us  [body(): pl.pallas_call(functools.partial(series_kernel, temps, dets, own, devices...]
    reshape x2, local copies, waits for them, and re-layouts: 2.39 us -> 4.31 us  [body(): shaped_s = strain.reshape(2, dets, rows, depth)]
where the time goes in v3:
time: 36.4 us; the launch traced here: 36.1 us
  Pallas kernels  14.1 us (39%)
  waiting for transfers between devices  8.47 us (23%)
  starting transfers between devices  7.43 us (20%)
  local copies, waits for them, and re-layouts  5.89 us (16%)
    all_to_all x1, waiting for transfers between devices, body(): lax.all_to_all(parts, ('filt', 'sky'), split_axis=0, concat_axis=0, tiled...  8.47 us
    all_to_all x1, starting transfers between devices, body(): lax.all_to_all(parts, ('filt', 'sky'), split_axis=0, concat_axis=0, tiled...  7.43 us
    pallas_call x1, Pallas kernels, body(): pl.pallas_call(functools.partial(sky_kernel, temps, dets, own, devices, c...  7.22 us
    pallas_call x1, Pallas kernels, body(): pl.pallas_call(functools.partial(series_kernel, temps, dets, own, devices...  6.45 us
    reshape x2, local copies, waits for them, and re-layouts, body(): shaped_s = strain.reshape(2, dets, rows, depth)  4.31 us
    reshape x1, local copies, waits for them, and re-layouts, body(): shaped_h = templates.reshape(2, temps, rows, depth)  1.52 us
  transfers between devices with their start and end apart: 1, of which 1 were waited for; matrix products, arithmetic and copies ran while one was open for 0% of the time, Pallas kernels for 1%

profile of v3, /device:TPU:0, one launch (start us, length us, event | category | flops | bytes accessed | tf_op | source)
XLA Modules:
  0.0 36.1 jit_solution(15002417275566351945)
XLA Ops:
  0.0 0.0 copy-start
  0.0 0.0 copy-start.5
  0.0 0.0 copy-start.7
  0.0 0.0 copy-start.8
  0.1 1.5 %reshape.7.templates = bf16[2,2,128,512]{3,2,1,0:T(8,128)(2,1)S(1)} reshape(bf16[2,2,65536]{2,1,0:T(2,128)(2,1)} %param.13) | data formatting | bytes 1048576 | tf_op jit(solution)/shard_map/reshape | solution.py:283
  1.6 3.1 %reshape.6 = bf16[2,3,128,512]{3,2,0,1:T(8,128)(2,1)} reshape(bf16[2,3,65536]{2,0,1:T(2,128)(2,1)} %param.12) | data formatting | bytes 1572864 | tf_op jit(solution)/shard_map/reshape | solution.py:282
  4.7 1.2 %copy.15.strain = bf16[2,3,128,512]{3,2,1,0:T(8,128)(2,1)S(1)} copy(bf16[2,3,128,512]{3,2,0,1:T(8,128)(2,1)} %reshape.6) | data formatting | bytes 1572864 | tf_op jit(solution)/shard_map/reshape | solution.py:282
  5.9 0.0 copy-done
  5.9 0.0 copy-done.1
  5.9 0.0 copy-done.2
  5.9 0.0 copy-done.3
  5.9 0.0 copy-done.4
  5.9 0.0 copy-done.5
  6.0 0.0 copy-done.7
  6.0 0.0 copy-done.8
  6.0 0.0 copy-start.9
  6.0 0.0 copy-start.6
  6.0 6.5 %series.1 = bf16[16,16,384]{2,1,0:T(8,128)(2,1)} custom-call(s32[2]{0:T(128)S(1)} %copy-done.8, bf16[2,3,128,512]{3,2,1,0:T(8,128)(2,1)S(1)} %copy.15.strain, bf16[2,2,128,512]{3,2,1,0:T(8,128)(2,1)S(1)} %reshape.7.templates, f32[4,128,256]{2,1,0:T(8,128)S(1)} %copy-done.2, f32[2,256,256]{2,1,0:T(8,128)S(1)} %copy-done.1, f32[2,256,256]{2,1,0:T(8,128)S(1)} %copy-done, ...), custom_call_target="tpu_custom_call" | custom-call | tf_op jit(solution)/shard_map/series/pallas_call | solution.py:284
  12.4 7.4 %all-to-all-start = ((bf16[16,16,384]{2,1,0:T(8,128)(2,1)}), bf16[16,16,384]{2,1,0:T(8,128)(2,1)S(1)}, u32[]{:S(2)}, u32[]{:S(2)}) async-start(bf16[16,16,384]{2,1,0:T(8,128)(2,1)} %series.1), calls=%async_computation | async-start | bytes 393216 | tf_op jit(solution)/shard_map/all_to_all | solution.py:301
  19.9 0.0 copy-done.9
  19.9 0.0 copy-done.6
  19.9 0.4 %weights.1 = bf16[3,640,512]{2,1,0:T(8,128)(2,1)S(1)} custom-call(s32[3,1536]{1,0:T(4,128)S(1)} %copy-done.6, bf16[2,3,1536]{2,1,0:T(4,128)(2,1)S(1)} %copy.16.antenna), custom_call_target="tpu_custom_call" | custom-call | flops 4194304 | bytes 3145728 | tf_op jit(solution)/shard_map/weights/pallas_call | solution.py:303
  20.4 8.5 %all-to-all-done.received = bf16[16,16,384]{2,1,0:T(8,128)(2,1)S(1)} async-done(((bf16[16,16,384]{2,1,0:T(8,128)(2,1)}), bf16[16,16,384]{2,1,0:T(8,128)(2,1)S(1)}, u32[]{:S(2)}, u32[]{:S(2)}) %all-to-all-start) | async-done | bytes 196640 | tf_op jit(solution)/shard_map/all_to_all | solution.py:301
  28.8 7.2 %sky.1 = f32[256,1536]{1,0:T(8,128)} custom-call(bf16[16,16,384]{2,1,0:T(8,128)(2,1)S(1)} %all-to-all-done.received, bf16[3,640,512]{2,1,0:T(8,128)(2,1)S(1)} %weights.1), custom_call_target="tpu_custom_call" | custom-call | tf_op jit(solution)/shard_map/sky/pallas_call | solution.py:312
  (5 shorter events, 0.0 us)
Async XLA Ops:
  0.0 5.9 %copy-start = (f32[2,256,256]{2,1,0:T(8,128)S(1)}, f32[2,256,256]{2,1,0:T(8,128)}, u32[]{:S(2)}) copy-start(f32[2,256,256]{2,1,0:T(8,128)} %constant.16.clone.col_step) | copy-start | bytes 1572868
  0.0 5.9 %copy-start.1 = (f32[2,256,256]{2,1,0:T(8,128)S(1)}, f32[2,256,256]{2,1,0:T(8,128)}, u32[]{:S(2)}) copy-start(f32[2,256,256]{2,1,0:T(8,128)} %constant.15.clone.col_first) | copy-start | bytes 1572868
  0.0 5.9 %copy-start.2 = (f32[4,128,256]{2,1,0:T(8,128)S(1)}, f32[4,128,256]{2,1,0:T(8,128)}, u32[]{:S(2)}) copy-start(f32[4,128,256]{2,1,0:T(8,128)} %constant.14.clone.start) | copy-start | bytes 1572868
  0.0 5.9 %copy-start.3 = (f32[2,128,256]{2,1,0:T(8,128)S(1)}, f32[2,128,256]{2,1,0:T(8,128)}, u32[]{:S(2)}) copy-start(f32[2,128,256]{2,1,0:T(8,128)} %constant.18.clone.row_step) | copy-start | bytes 786436
  0.0 5.9 %copy-start.4 = (f32[2,128,256]{2,1,0:T(8,128)S(1)}, f32[2,128,256]{2,1,0:T(8,128)}, u32[]{:S(2)}) copy-start(f32[2,128,256]{2,1,0:T(8,128)} %constant.17.clone.row_first) | copy-start | bytes 786436
  0.0 5.9 %copy-start.5 = (bf16[256,256]{1,0:T(8,128)(2,1)S(1)}, bf16[256,256]{1,0:T(8,128)(2,1)}, u32[]{:S(2)}) copy-start(bf16[256,256]{1,0:T(8,128)(2,1)} %constant.20.clone.flip) | copy-start | bytes 393220
  0.0 5.9 %copy-start.7 = (f32[8,4,128]{2,1,0:T(4,128)S(1)}, f32[8,4,128]{2,1,0:T(4,128)}, u32[]{:S(2)}) copy-start(f32[8,4,128]{2,1,0:T(4,128)} %constant.19.clone.offset) | copy-start | bytes 49156
  0.0 5.9 %copy-start.8 = (s32[2]{0:T(128)S(1)}, s32[2]{0:T(128)}, u32[]{:S(2)}) copy-start(s32[2]{0:T(128)} %lengths.1) | copy-start | bytes 28
  6.0 13.9 %copy-start.9 = (bf16[2,3,1536]{2,0,1:T(2,128)(2,1)S(1)}, bf16[2,3,1536]{2,0,1:T(2,128)(2,1)}, u32[]{:S(2)}) copy-start(bf16[2,3,1536]{2,0,1:T(2,128)(2,1)} %param.15) | copy-start | bytes 55300
  6.0 13.9 %copy-start.6 = (s32[3,1536]{1,0:T(4,128)S(1)}, s32[3,1536]{1,0:T(4,128)}, u32[]{:S(2)}) copy-start(s32[3,1536]{1,0:T(4,128)} %delays.1) | copy-start | bytes 55300
  12.4 16.4 %all-to-all-start = ((bf16[16,16,384]{2,1,0:T(8,128)(2,1)}), bf16[16,16,384]{2,1,0:T(8,128)(2,1)S(1)}, u32[]{:S(2)}, u32[]{:S(2)}) async-start(bf16[16,16,384]{2,1,0:T(8,128)(2,1)} %series.1), calls=%async_computation | async-start | bytes 393216 | tf_op jit(solution)/shard_map/all_to_all | solution.py:301

commit v4 on v3

--- a/solution.py
+++ b/solution.py
@@ -59,7 +59,7 @@
     pos = lax.axis_index("filt")
     for r in range(2):
         for d in range(dets):
-            turned = jnp.dot(strain[r, d, :, :side], flip[...], preferred_element_type=jnp.float32)
+            turned = jnp.dot(strain[d, r, :, :side], flip[...], preferred_element_type=jnp.float32)
             back_s[r, d] = turned.astype(jnp.bfloat16)
         for k in range(temps):
             turned = jnp.dot(templates[r, k, :, :side], flip[...], preferred_element_type=jnp.float32)
@@ -72,8 +72,8 @@
         row_bin = (pos * rows + first) * depth + lax.broadcasted_iota(jnp.int32, (ROWS, side), 0) * depth
         lane = lax.broadcasted_iota(jnp.int32, (ROWS, side), 1)
         bins = (row_bin + side + lane, row_bin + side - 1 - lane)
-        s_re = [(strain[0, d, here, side:].astype(jnp.float32), back_s[0, d, here, :].astype(jnp.float32)) for d in range(dets)]
-        s_im = [(strain[1, d, here, side:].astype(jnp.float32), back_s[1, d, here, :].astype(jnp.float32)) for d in range(dets)]
+        s_re = [(strain[d, 0, here, side:].astype(jnp.float32), back_s[0, d, here, :].astype(jnp.float32)) for d in range(dets)]
+        s_im = [(strain[d, 1, here, side:].astype(jnp.float32), back_s[1, d, here, :].astype(jnp.float32)) for d in range(dets)]
         added = []
         for k in range(temps):
             energy = norms[k]
@@ -279,7 +279,7 @@
     count = temps * dets
     vmem = pl.BlockSpec(memory_space=pltpu.VMEM)
     smem = pl.BlockSpec(memory_space=pltpu.SMEM)
-    shaped_s = strain.reshape(2, dets, rows, depth)
+    shaped_s = strain.reshape(2, dets, rows, depth).transpose(1, 0, 2, 3)
     shaped_h = templates.reshape(2, temps, rows, depth)
     parts = pl.pallas_call(
         functools.partial(series_kernel, temps, dets, own, devices, copies, half_tiles),

time: 36.4 us -> 35.1 us (0.964)
  waiting for transfers between devices: 8.47 us -> 7.03 us
    unnamed x21 -> x19, local copies, waits for them, and re-layouts: 0.06 us -> 2.15 us
    reshape x2 -> x1, local copies, waits for them, and re-layouts: 4.31 us -> 2.32 us  [body(): shaped_s = strain.reshape(2, dets, rows, depth).transpose(1, 0, 2, 3)]
    all_to_all x1, waiting for transfers between devices: 8.47 us -> 7.03 us  [body(): lax.all_to_all(parts, ('filt', 'sky'), split_axis=0, concat_axis=0, tiled...]
  transfers between devices with their start and end apart: 1 -> 1, of which waited for: 1 -> 1; matrix products, arithmetic and copies ran while one was open for 0% -> 2% of each run, Pallas kernels for 1% -> 1%
where the time goes in v4:
time: 35.1 us; the launch traced here: 34.7 us
  Pallas kernels  14.1 us (40%)
  starting transfers between devices  7.43 us (21%)
  waiting for transfers between devices  7.03 us (20%)
  local copies, waits for them, and re-layouts  5.99 us (17%)
    all_to_all x1, starting transfers between devices, body(): lax.all_to_all(parts, ('filt', 'sky'), split_axis=0, concat_axis=0, tiled...  7.43 us
    pallas_call x1, Pallas kernels, body(): pl.pallas_call(functools.partial(sky_kernel, temps, dets, own, devices, c...  7.22 us
    all_to_all x1, waiting for transfers between devices, body(): lax.all_to_all(parts, ('filt', 'sky'), split_axis=0, concat_axis=0, tiled...  7.03 us
    pallas_call x1, Pallas kernels, body(): pl.pallas_call(functools.partial(series_kernel, temps, dets, own, devices...  6.44 us
    reshape x1, local copies, waits for them, and re-layouts, body(): shaped_s = strain.reshape(2, dets, rows, depth).transpose(1, 0, 2, 3)  2.32 us
    unnamed x19, local copies, waits for them, and re-layouts  2.15 us
    reshape x1, local copies, waits for them, and re-layouts, body(): shaped_h = templates.reshape(2, temps, rows, depth)  1.52 us
  transfers between devices with their start and end apart: 1, of which 1 were waited for; matrix products, arithmetic and copies ran while one was open for 2% of the time, Pallas kernels for 1%

profile of v4, /device:TPU:0, one launch (start us, length us, event | category | flops | bytes accessed | tf_op | source)
XLA Modules:
  0.0 34.7 jit_solution(1296655407157469249)
XLA Ops:
  0.0 0.0 copy-start.5
  0.0 0.0 copy-start.7
  0.0 0.0 copy-start.3
  0.0 0.0 copy-start.1
  0.0 0.0 copy-start.2
  0.0 1.5 %reshape.7.templates = bf16[2,2,128,512]{3,2,1,0:T(8,128)(2,1)S(1)} reshape(bf16[2,2,65536]{2,1,0:T(2,128)(2,1)} %param.13) | data formatting | bytes 1048576 | tf_op jit(solution)/shard_map/reshape | solution.py:283
  1.6 2.3 %reshape.6 = bf16[2,3,128,512]{3,2,0,1:T(8,128)(2,1)S(1)} reshape(bf16[2,3,65536]{2,0,1:T(2,128)(2,1)} %param.12) | data formatting | bytes 1572864 | tf_op jit(solution)/shard_map/reshape | solution.py:282
  3.9 0.0 copy-done.5
  3.9 0.0 copy-done.7
  3.9 0.0 copy-done.3
  3.9 0.0 copy-done.4
  3.9 0.0 copy-done
  3.9 0.0 copy-done.1
  4.0 0.0 copy-done.2
  4.0 0.0 copy-start.8
  4.0 0.6 %copy-done.8 = s32[2]{0:T(128)S(1)} copy-done((s32[2]{0:T(128)S(1)}, s32[2]{0:T(128)}, u32[]{:S(2)}) %copy-start.8) | copy-done | bytes 32
  4.6 6.4 %series.1 = bf16[16,16,384]{2,1,0:T(8,128)(2,1)} custom-call(s32[2]{0:T(128)S(1)} %copy-done.8, bf16[3,2,128,512]{3,2,1,0:T(8,128)(2,1)S(1)} %bitcast.4, bf16[2,2,128,512]{3,2,1,0:T(8,128)(2,1)S(1)} %reshape.7.templates, f32[4,128,256]{2,1,0:T(8,128)S(1)} %copy-done.2, f32[2,256,256]{2,1,0:T(8,128)S(1)} %copy-done.1, f32[2,256,256]{2,1,0:T(8,128)S(1)} %copy-done, ...), custom_call_target="tpu_custom_call" | custom-call | tf_op jit(solution)/shard_map/series/pallas_call | solution.py:284
  11.1 7.4 %all-to-all-start = ((bf16[16,16,384]{2,1,0:T(8,128)(2,1)}), bf16[16,16,384]{2,1,0:T(8,128)(2,1)S(1)}, u32[]{:S(2)}, u32[]{:S(2)}) async-start(bf16[16,16,384]{2,1,0:T(8,128)(2,1)} %series.1), calls=%async_computation | async-start | bytes 393216 | tf_op jit(solution)/shard_map/all_to_all | solution.py:301
  18.5 0.7 %copy.13.antenna = bf16[2,3,1536]{2,1,0:T(4,128)(2,1)S(1)} copy(bf16[2,3,1536]{2,0,1:T(2,128)(2,1)} %param.15) | data formatting | bytes 36864 | tf_op args[3]
  19.2 0.0 copy-start.6
  19.3 0.7 %copy-done.6 = s32[3,1536]{1,0:T(4,128)S(1)} copy-done((s32[3,1536]{1,0:T(4,128)S(1)}, s32[3,1536]{1,0:T(4,128)}, u32[]{:S(2)}) %copy-start.6) | copy-done | bytes 18456
  20.0 0.4 %weights.1 = bf16[3,640,512]{2,1,0:T(8,128)(2,1)S(1)} custom-call(s32[3,1536]{1,0:T(4,128)S(1)} %copy-done.6, bf16[2,3,1536]{2,1,0:T(4,128)(2,1)S(1)} %copy.13.antenna), custom_call_target="tpu_custom_call" | custom-call | flops 4194304 | bytes 3145728 | tf_op jit(solution)/shard_map/weights/pallas_call | solution.py:303
  20.4 7.0 %all-to-all-done.received = bf16[16,16,384]{2,1,0:T(8,128)(2,1)S(1)} async-done(((bf16[16,16,384]{2,1,0:T(8,128)(2,1)}), bf16[16,16,384]{2,1,0:T(8,128)(2,1)S(1)}, u32[]{:S(2)}, u32[]{:S(2)}) %all-to-all-start) | async-done | bytes 196640 | tf_op jit(solution)/shard_map/all_to_all | solution.py:301
  27.5 7.2 %sky.1 = f32[256,1536]{1,0:T(8,128)} custom-call(bf16[16,16,384]{2,1,0:T(8,128)(2,1)S(1)} %all-to-all-done.received, bf16[3,640,512]{2,1,0:T(8,128)(2,1)S(1)} %weights.1), custom_call_target="tpu_custom_call" | custom-call | tf_op jit(solution)/shard_map/sky/pallas_call | solution.py:312
  (2 shorter events, 0.0 us)
Async XLA Ops:
  0.0 3.9 %copy-start.5 = (bf16[256,256]{1,0:T(8,128)(2,1)S(1)}, bf16[256,256]{1,0:T(8,128)(2,1)}, u32[]{:S(2)}) copy-start(bf16[256,256]{1,0:T(8,128)(2,1)} %constant.20.clone.flip) | copy-start | bytes 393220
  0.0 3.9 %copy-start.7 = (f32[8,4,128]{2,1,0:T(4,128)S(1)}, f32[8,4,128]{2,1,0:T(4,128)}, u32[]{:S(2)}) copy-start(f32[8,4,128]{2,1,0:T(4,128)} %constant.19.clone.offset) | copy-start | bytes 49156
  0.0 3.9 %copy-start.3 = (f32[2,128,256]{2,1,0:T(8,128)S(1)}, f32[2,128,256]{2,1,0:T(8,128)}, u32[]{:S(2)}) copy-start(f32[2,128,256]{2,1,0:T(8,128)} %constant.18.clone.row_step) | copy-start | bytes 786436
  0.0 3.9 %copy-start.4 = (f32[2,128,256]{2,1,0:T(8,128)S(1)}, f32[2,128,256]{2,1,0:T(8,128)}, u32[]{:S(2)}) copy-start(f32[2,128,256]{2,1,0:T(8,128)} %constant.17.clone.row_first) | copy-start | bytes 786436
  0.0 3.9 %copy-start = (f32[2,256,256]{2,1,0:T(8,128)S(1)}, f32[2,256,256]{2,1,0:T(8,128)}, u32[]{:S(2)}) copy-start(f32[2,256,256]{2,1,0:T(8,128)} %constant.16.clone.col_step) | copy-start | bytes 1572868
  0.0 3.9 %copy-start.1 = (f32[2,256,256]{2,1,0:T(8,128)S(1)}, f32[2,256,256]{2,1,0:T(8,128)}, u32[]{:S(2)}) copy-start(f32[2,256,256]{2,1,0:T(8,128)} %constant.15.clone.col_first) | copy-start | bytes 1572868
  0.0 3.9 %copy-start.2 = (f32[4,128,256]{2,1,0:T(8,128)S(1)}, f32[4,128,256]{2,1,0:T(8,128)}, u32[]{:S(2)}) copy-start(f32[4,128,256]{2,1,0:T(8,128)} %constant.14.clone.start) | copy-start | bytes 1572868
  4.0 0.7 %copy-start.8 = (s32[2]{0:T(128)S(1)}, s32[2]{0:T(128)}, u32[]{:S(2)}) copy-start(s32[2]{0:T(128)} %lengths.1) | copy-start | bytes 28
  11.1 16.4 %all-to-all-start = ((bf16[16,16,384]{2,1,0:T(8,128)(2,1)}), bf16[16,16,384]{2,1,0:T(8,128)(2,1)S(1)}, u32[]{:S(2)}, u32[]{:S(2)}) async-start(bf16[16,16,384]{2,1,0:T(8,128)(2,1)} %series.1), calls=%async_computation | async-start | bytes 393216 | tf_op jit(solution)/shard_map/all_to_all | solution.py:301
  19.2 0.7 %copy-start.6 = (s32[3,1536]{1,0:T(4,128)S(1)}, s32[3,1536]{1,0:T(4,128)}, u32[]{:S(2)}) copy-start(s32[3,1536]{1,0:T(4,128)} %delays.1) | copy-start | bytes 55300
